TPU v7x, 32 devices: a whole 2x2x4 slice. The times are simulated.
32 devices in a mesh: grp: 2 (over x), gx: 4 (over z), gy: 4 (over y, core).
Axes of the slice: x: 2, y: 2, z: 4, core: 2. Of those that a mesh axis runs over, the one named last changes fastest.
Arguments:
- theta_anomaly: float32 [192, 64, 128], P(('grp', 'gx'), 'gy'), may hold values from -4 to 4
- humidity_ratio: float32 [192, 64, 128], P(('grp', 'gx'), 'gy'), may hold values from 0.6 to 1.4
- zonal_velocity: float32 [192, 64, 128], P(('grp', 'gx'), 'gy'), may hold values from -1.8 to 1.8
- meridional_velocity: float32 [192, 64, 128], P(('grp', 'gx'), 'gy'), may hold values from -1.8 to 1.8
- vertical_velocity: float32 [192, 64, 128], P(('grp', 'gx'), 'gy'), may hold values from -1.8 to 1.8
- patch_processor_map: int32 [8, 4, 8], P(('grp', 'gx'), 'gy'), may hold values from 0 to 3, as said below
- particle_bucket_population: int32 [8, 4, 8], P(('grp', 'gx'), 'gy'), may hold values from 0 to 1024, as said below
- particle_size_quadratic: float32 [8, 4, 8, 1024], P(('grp', 'gx'), 'gy'), may hold values from 0.25 to 4
- represented_number: float32 [8, 4, 8, 1024], P(('grp', 'gx'), 'gy'), may hold values from 0.5 to 2
- particle_location_number: int32 [8, 4, 8, 1024], P(('grp', 'gx'), 'gy'), may hold values from 48 to 6095, as said below
Outputs:
- final_temperature: float32 [192, 64, 128], P(('grp', 'gx'), 'gy')
- final_vapour: float32 [192, 64, 128], P(('grp', 'gx'), 'gy')
- final_east: float32 [192, 64, 128], P(('grp', 'gx'), 'gy')
- final_north: float32 [192, 64, 128], P(('grp', 'gx'), 'gy')
- final_vertical: float32 [192, 64, 128], P(('grp', 'gx'), 'gy')
- final_size_quadratic: float32 [8, 4, 8, 1024], P(('grp', 'gx'), 'gy')
Inputs may be any that keep to these rules, and one draw needn't show every extreme that they name: `patch_processor_map`: entry [a, y, b] is the index along gx of the device in the same row (same grp half, same gy) that holds the droplets of column block b of device (a, y). Different blocks of one device go to different owners, so one device sends at most 2 blocks to one owner; in every row some owner holds 2 blocks from every device of the row. `particle_bucket_population`: entry [a, y, r] counts the live droplets of slot r = s x 2 + t of the owner (a, y); they are the first ones of the slot. A slot that receives no block has none; every slot of an owner that holds 2 blocks from every device is full. `particle_location_number`: the cell within the slot's block, column 128 + level, with levels from 48 to 79. Within a slot the live droplets are sorted by column, and so are the others.
All inputs are finite; a program needn't handle non-finite values.
Results may differ from a plain program's by a relative error of at most 0.0003.
Values sent between devices are 32-bit elements; how exact they have to be, the bound alone decides.
A program may use at most 64 MiB of HBM per device.

v0:
```python
import jax
import jax.numpy as jnp
from jax import lax
from jax.sharding import PartitionSpec as P

NBD = 8
NSUB = 4
ITERS = 4
TIME_INCREMENT = 0.15
THERMAL_LIFT = 0.5
HUMID_LIFT = 0.3
HELMHOLTZ = 0.001
CLAUSIUS_FACTOR = 0.2
GROWTH = 0.5
GROWTH_SLOPE = 0.1
SUB_STEP = 0.25
CURVATURE = 0.05
FLOOR_SQUARE = 0.04
CONDENSE = 0.2
PHASE_WARMING = 2.5


def with_halo(block, sides, width):
    for axis, dim in sides:
        count = lax.axis_size(axis)
        forward = [(i, i + 1) for i in range(count - 1)]
        forward.append((count - 1, 0))
        backward = [(target, source) for source, target in forward]
        low = lax.ppermute(
            lax.slice_in_dim(block, block.shape[dim] - width, None, axis=dim), axis, forward
        )
        high = lax.ppermute(lax.slice_in_dim(block, 0, width, axis=dim), axis, backward)
        block = jnp.concatenate([low, block, high], axis=dim)
    return block


def surround(stacked):
    return with_halo(stacked, ((("grp", "gx"), 1), ("gy", 2)), 1)


def beside(padded):
    return (
        padded[:, 2:, 1:-1, :],
        padded[:, :-2, 1:-1, :],
        padded[:, 1:-1, 2:, :],
        padded[:, 1:-1, :-2, :],
    )


def level_above(values):
    return jnp.concatenate([values[..., 1:], jnp.zeros_like(values[..., :1])], axis=-1)


def level_below(values):
    return jnp.concatenate([jnp.zeros_like(values[..., :1]), values[..., :-1]], axis=-1)


def profiles(layer_altitudes):
    heights = jnp.arange(layer_altitudes, dtype=jnp.float32)
    midpoint_mass_per_volume = jnp.exp(-(heights + 0.5) / layer_altitudes)
    interface_mass_per_volume = jnp.where(
        heights < layer_altitudes - 1, jnp.exp(-(heights + 1.0) / layer_altitudes), 0.0
    )
    return (midpoint_mass_per_volume, interface_mass_per_volume)


def operate(values, midpoint_mass_per_volume, interface_mass_per_volume):
    east_side, west_side, north_side, south_side = beside(surround(values[None]))
    return (
        midpoint_mass_per_volume
        * ((4.0 + HELMHOLTZ) * values - east_side[0] - west_side[0] - north_side[0] - south_side[0])
        + interface_mass_per_volume * (values - level_above(values))
        + level_below(interface_mass_per_volume) * (values - level_below(values))
    )


def both_sums(residual, applied):
    return lax.psum(
        (jnp.sum(residual * residual), jnp.sum(residual * applied)), ("grp", "gx", "gy")
    )


def solve_pressure(right_side, midpoint_mass_per_volume, interface_mass_per_volume):
    potential = jnp.zeros_like(right_side)
    residual = right_side
    applied = operate(residual, midpoint_mass_per_volume, interface_mass_per_volume)
    norm_now, product = both_sums(residual, applied)
    step_length = norm_now / product
    direction, along_dir = (residual, applied)
    for iteration in range(ITERS):
        potential = potential + step_length * direction
        residual = residual - step_length * along_dir
        if iteration + 1 < ITERS:
            applied = operate(residual, midpoint_mass_per_volume, interface_mass_per_volume)
            norm_next, product = both_sums(residual, applied)
            beta_ratio = norm_next / norm_now
            step_length = norm_next / (product - beta_ratio * norm_next / step_length)
            direction = residual + beta_ratio * direction
            along_dir = applied + beta_ratio * along_dir
            norm_now = norm_next
    return potential


def momentum_update(
    theta_anomaly,
    humidity_ratio,
    zonal_velocity,
    meridional_velocity,
    vertical_velocity,
    midpoint_mass_per_volume,
    interface_mass_per_volume,
):
    raised_airmass = vertical_velocity + TIME_INCREMENT * (
        THERMAL_LIFT * theta_anomaly + HUMID_LIFT * humidity_ratio
    )
    east_side, west_side, north_side, south_side = beside(
        surround(jnp.stack([zonal_velocity, meridional_velocity]))
    )
    divergence = midpoint_mass_per_volume * (
        (east_side[0] - west_side[0]) * 0.5 + (north_side[1] - south_side[1]) * 0.5
    ) + 0.5 * (
        level_above(midpoint_mass_per_volume * raised_airmass)
        - level_below(midpoint_mass_per_volume * raised_airmass)
    )
    potential = solve_pressure(
        -divergence / TIME_INCREMENT, midpoint_mass_per_volume, interface_mass_per_volume
    )
    pot_east, pot_west, pot_north, pot_south = beside(surround(potential[None]))
    zonal_velocity = zonal_velocity - TIME_INCREMENT * 0.5 * (pot_east[0] - pot_west[0])
    meridional_velocity = meridional_velocity - TIME_INCREMENT * 0.5 * (pot_north[0] - pot_south[0])
    vertical_velocity = raised_airmass - TIME_INCREMENT * 0.5 * (
        level_above(potential) - level_below(potential)
    )
    scalar_quantities = jnp.stack([theta_anomaly, humidity_ratio])
    tra_east, tra_west, tra_north, tra_south = beside(surround(scalar_quantities))
    lower_level = jnp.concatenate(
        [scalar_quantities[..., :1], scalar_quantities[..., :-1]], axis=-1
    )
    upper_level = jnp.concatenate(
        [scalar_quantities[..., 1:], scalar_quantities[..., -1:]], axis=-1
    )
    tendency = (
        jnp.maximum(zonal_velocity, 0.0) * (scalar_quantities - tra_west)
        + jnp.minimum(zonal_velocity, 0.0) * (tra_east - scalar_quantities)
        + jnp.maximum(meridional_velocity, 0.0) * (scalar_quantities - tra_south)
        + jnp.minimum(meridional_velocity, 0.0) * (tra_north - scalar_quantities)
        + jnp.maximum(vertical_velocity, 0.0) * (scalar_quantities - lower_level)
        + jnp.minimum(vertical_velocity, 0.0) * (upper_level - scalar_quantities)
    )
    moved = scalar_quantities - TIME_INCREMENT * tendency
    return (moved[0], moved[1], zonal_velocity, meridional_velocity, vertical_velocity)


def grow_droplets(supersat_ratio, warmth, particle_size_quadratic, represented_number, alive_mask):
    growth_rate = GROWTH * jnp.exp(GROWTH_SLOPE * warmth)
    square_now = particle_size_quadratic
    for substep in range(NSUB):
        square_now = jnp.maximum(
            square_now
            + 2.0 * SUB_STEP * growth_rate * (supersat_ratio - CURVATURE / jnp.sqrt(square_now)),
            FLOOR_SQUARE,
        )
    grown_square = jnp.where(alive_mask, square_now, particle_size_quadratic)
    mass_change = jnp.where(
        alive_mask,
        represented_number
        * (
            grown_square * jnp.sqrt(grown_square)
            - particle_size_quadratic * jnp.sqrt(particle_size_quadratic)
        ),
        0.0,
    )
    return (grown_square, mass_change)


def grow_rows(columns, radius_squared_rows, mult_rows, local_cell, alive_mask):
    row_count = columns.shape[0]
    thermal_couple = columns.reshape(row_count, 2, -1)
    cells_per = thermal_couple.shape[2]
    supersat_ratio = jnp.take_along_axis(thermal_couple[:, 0], local_cell, axis=1)
    warmth = jnp.take_along_axis(thermal_couple[:, 1], local_cell, axis=1)
    grown_square, mass_change = grow_droplets(
        supersat_ratio, warmth, radius_squared_rows, mult_rows, alive_mask
    )
    flat_cell = local_cell + cells_per * jnp.arange(row_count, dtype=jnp.int32)[:, None]
    liquid_content = CONDENSE * jax.ops.segment_sum(
        mass_change.reshape(-1), flat_cell.reshape(-1), num_segments=row_count * cells_per
    )
    return (grown_square, liquid_content.reshape(row_count, cells_per))


def into_patches(values):
    domain_length_east, domain_length_north, layer_depth = values.shape
    shaped = values.reshape(domain_length_east, NBD, domain_length_north // NBD, layer_depth)
    return shaped.transpose(1, 0, 2, 3).reshape(NBD, -1)


def from_blocks(blocks, domain_length_east, domain_length_north, layer_depth):
    shaped = blocks.reshape(NBD, domain_length_east, domain_length_north // NBD, layer_depth)
    return shaped.transpose(1, 0, 2, 3).reshape(
        domain_length_east, domain_length_north, layer_depth
    )


def routing_plan(owner_row, slots, row_count):
    row_index = jnp.arange(row_count, dtype=jnp.int32)[:, None]
    block_index = jnp.arange(owner_row.shape[0], dtype=jnp.int32)[None, :]
    matches = (owner_row[None, :] == row_index // slots) & (
        block_index % slots == row_index % slots
    )
    return matches.astype(jnp.float32)


def on_device(
    theta_anomaly,
    humidity_ratio,
    zonal_velocity,
    meridional_velocity,
    vertical_velocity,
    patch_processor_map,
    particle_bucket_population,
    particle_size_quadratic,
    represented_number,
    particle_location_number,
):
    domain_length_east, domain_length_north, layer_altitudes = theta_anomaly.shape
    midpoint_mass_per_volume, interface_mass_per_volume = profiles(layer_altitudes)
    radius_squared_rows = particle_size_quadratic[0, 0]
    mult_rows = represented_number[0, 0]
    cell_rows = particle_location_number[0, 0]
    count_rows = particle_bucket_population[0, 0]
    row_count = radius_squared_rows.shape[0]
    slots = row_count // lax.axis_size("gx")
    routing = routing_plan(patch_processor_map[0, 0], slots, row_count)
    layer_low = 0
    layer_depth = layer_altitudes - layer_low
    local_cell = (
        cell_rows // layer_altitudes * layer_depth + cell_rows % layer_altitudes - layer_low
    )
    alive_mask = (
        jnp.arange(radius_squared_rows.shape[1], dtype=jnp.int32)[None, :] < count_rows[:, None]
    )
    advected_theta, advected_humidity, zonal_velocity, meridional_velocity, vertical_velocity = (
        momentum_update(
            theta_anomaly,
            humidity_ratio,
            zonal_velocity,
            meridional_velocity,
            vertical_velocity,
            midpoint_mass_per_volume,
            interface_mass_per_volume,
        )
    )
    supersat_ratio = advected_humidity * jnp.exp(-CLAUSIUS_FACTOR * advected_theta) - 1.0
    thermal_couple = jnp.stack(
        [into_patches(supersat_ratio), into_patches(advected_theta)], axis=1
    ).reshape(NBD, -1)
    columns = jnp.dot(routing, thermal_couple, precision=lax.Precision.HIGHEST)
    arrived_columns = lax.all_to_all(columns, "gx", split_axis=0, concat_axis=0, tiled=True)
    radius_squared_rows, owner_rows = grow_rows(
        arrived_columns, radius_squared_rows, mult_rows, local_cell, alive_mask
    )
    condensed_rows = lax.all_to_all(owner_rows, "gx", split_axis=0, concat_axis=0, tiled=True)
    liquid_content = from_blocks(
        jnp.dot(routing.T, condensed_rows, precision=lax.Precision.HIGHEST),
        domain_length_east,
        domain_length_north,
        layer_depth,
    )
    theta_anomaly = advected_theta + PHASE_WARMING * liquid_content
    humidity_ratio = advected_humidity - liquid_content
    return (
        theta_anomaly,
        humidity_ratio,
        zonal_velocity,
        meridional_velocity,
        vertical_velocity,
        radius_squared_rows[None, None],
    )


def solution(mesh):
    placed = (
        P(("grp", "gx"), "gy", None),
        P(("grp", "gx"), "gy", None),
        P(("grp", "gx"), "gy", None),
        P(("grp", "gx"), "gy", None),
        P(("grp", "gx"), "gy", None),
        P(("grp", "gx"), "gy", None),
        P(("grp", "gx"), "gy", None),
        P(("grp", "gx"), "gy", None, None),
        P(("grp", "gx"), "gy", None, None),
        P(("grp", "gx"), "gy", None, None),
    )
    return jax.shard_map(
        on_device,
        mesh=mesh,
        in_specs=placed,
        out_specs=(
            P(("grp", "gx"), "gy", None),
            P(("grp", "gx"), "gy", None),
            P(("grp", "gx"), "gy", None),
            P(("grp", "gx"), "gy", None),
            P(("grp", "gx"), "gy", None),
            P(("grp", "gx"), "gy", None, None),
        ),
        check_vma=False,
    )
```

profile of v0, /device:TPU:0, one launch (start us, length us, event | category | flops | bytes accessed | tf_op | source)
XLA Modules:
  0.0 446.6 jit_solution(3342073956511347936)
XLA Ops:
  0.7 0.8 pad_maximum_fusion.74
  1.5 6.0 %collective-permute-start = (f32[2,1,16,128]{3,2,1,0:T(8,128)S(1)}, f32[2,1,16,128]{3,2,1,0:T(8,128)S(1)}, u32[]{:S(2)}, u32[]{:S(2)}) collective-permute-start(f32[2,1,16,128]{3,2,1,0:T(8,128)S(1)} %get-tuple-element.59), channel_id=1, source_target_pairs={{4,0},{8,4},{12,8},{16,12},{20,16},{24,20},{28,24},{0,28},{5,1},{9... | collective-permute-start | bytes 49160 | tf_op jit(solution)/shard_map/ppermute | solution.py:32
  8.3 4.7 %collective-permute-start.23 = (f32[2,1,16,128]{3,1,2,0:T(1,128)}, f32[2,1,16,128]{3,1,2,0:T(1,128)}, u32[]{:S(2)}, u32[]{:S(2)}) collective-permute-start(f32[2,1,16,128]{3,1,2,0:T(1,128)} %get-tuple-element.65), channel_id=1, source_target_pairs={{4,0},{8,4},{12,8},{16,12},{20,16},{24,20},{28,24},{0,28},{5,1},{9... | collective-permute-start | bytes 49160 | tf_op jit(solution)/shard_map/ppermute | solution.py:32
  15.1 1.1 collective-permute-done.2
  16.2 2.0 collective-permute-done.3
  18.4 2.0 collective-permute-start.4
  20.5 1.5 collective-permute-done.4
  22.1 4.7 %collective-permute-done.5 = f32[1,1,16,128]{3,2,1,0:T(8,128)S(1)} collective-permute-done((f32[1,1,16,128]{3,2,1,0:T(8,128)S(1)}, f32[1,1,16,128]{3,2,1,0:T(8,128)S(1)}, u32[]{:S(2)}, u32[]{:S(2)}) %collective-permute-start.5) | collective-permute-done | bytes 8224 | tf_op jit(solution)/shard_map/ppermute | solution.py:29
  27.5 0.8 collective-permute-done.6
  28.3 1.8 collective-permute-done.7
  30.0 0.8 multiply_reduce_fusion.5
  30.8 37.1 %all-reduce.15 = (f32[]{:T(128)}, f32[]{:T(128)}) all-reduce(f32[]{:T(128)} %get-tuple-element.26, f32[]{:T(128)} %get-tuple-element.25), channel_id=1, replica_groups=mesh['grp'=2,'gx'=4,'gy'=4] {'grp','gx','gy'}, use_global_device_ids=true, to_apply=%region_1.2 | all-reduce | flops 2 | bytes 16 | tf_op jit(solution)/shard_map/psum | solution.py:78
  69.3 4.0 collective-permute-start.8
  73.5 1.2 collective-permute-done.8
  74.7 5.0 %collective-permute-done.9 = f32[1,1,16,128]{3,2,1,0:T(8,128)S(1)} collective-permute-done((f32[1,1,16,128]{3,2,1,0:T(8,128)S(1)}, f32[1,1,16,128]{3,2,1,0:T(8,128)S(1)}, u32[]{:S(2)}, u32[]{:S(2)}) %collective-permute-start.9) | collective-permute-done | bytes 8224 | tf_op jit(solution)/shard_map/ppermute | solution.py:29
  80.4 0.8 collective-permute-done.10
  81.2 1.9 collective-permute-done.11
  83.8 37.2 %all-reduce.14 = (f32[]{:T(128)}, f32[]{:T(128)}) all-reduce(f32[]{:T(128)} %get-tuple-element.24, f32[]{:T(128)} %get-tuple-element.23), channel_id=1, replica_groups=mesh['grp'=2,'gx'=4,'gy'=4] {'grp','gx','gy'}, use_global_device_ids=true, to_apply=%region_5.6 | all-reduce | flops 2 | bytes 16 | tf_op jit(solution)/shard_map/psum | solution.py:78
  125.7 4.0 collective-permute-start.12
  129.7 0.9 fusion.2
  131.9 4.2 collective-permute-done.13
  136.8 0.8 collective-permute-done.14
  137.6 1.9 collective-permute-done.15
  139.5 1.5 multiply_reduce_fusion.1
  141.0 37.2 %all-reduce.13 = (f32[]{:T(128)}, f32[]{:T(128)}) all-reduce(f32[]{:T(128)} %get-tuple-element.22, f32[]{:T(128)} %get-tuple-element.21), channel_id=1, replica_groups=mesh['grp'=2,'gx'=4,'gy'=4] {'grp','gx','gy'}, use_global_device_ids=true, to_apply=%region_9.10 | all-reduce | flops 2 | bytes 16 | tf_op jit(solution)/shard_map/psum | solution.py:78
  182.0 1.0 multiply_subtract_fusion.1
  183.0 4.0 collective-permute-start.16
  187.0 1.3 pad_maximum_fusion.69
  188.4 1.7 collective-permute-start.27
  190.1 3.3 collective-permute-done.17
  194.9 2.2 collective-permute-done.19
  197.2 0.8 fusion.37
  197.9 37.4 %all-reduce.12 = (f32[]{:T(128)}, f32[]{:T(128)}) all-reduce(f32[]{:T(128)} %get-tuple-element.20, f32[]{:T(128)} %get-tuple-element.19), channel_id=1, replica_groups=mesh['grp'=2,'gx'=4,'gy'=4] {'grp','gx','gy'}, use_global_device_ids=true, to_apply=%region_13.14 | all-reduce | flops 2 | bytes 16 | tf_op jit(solution)/shard_map/psum | solution.py:78
  239.5 4.0 collective-permute-start.20
  243.6 1.2 collective-permute-done.20
  244.8 5.0 %collective-permute-done.21 = f32[1,1,16,128]{3,2,1,0:T(8,128)S(1)} collective-permute-done((f32[1,1,16,128]{3,2,1,0:T(8,128)S(1)}, f32[1,1,16,128]{3,2,1,0:T(8,128)S(1)}, u32[]{:S(2)}, u32[]{:S(2)}) %collective-permute-start.21) | collective-permute-done | bytes 8224 | tf_op jit(solution)/shard_map/ppermute | solution.py:29
  251.3 1.9 collective-permute-done.25
  254.4 0.8 copy-done.4
  255.2 1.2 fusion.10
  257.4 1.3 fusion.110
  258.6 3.8 all-to-all-start
  262.8 11.6 %all-to-all-done = f32[4,2,12288]{2,1,0:T(2,128)S(1)} async-done(((f32[4,2,12288]{2,1,0:T(2,128)}), f32[4,2,12288]{2,1,0:T(2,128)S(1)}, u32[]{:S(2)}, u32[]{:S(2)}) %all-to-all-start) | async-done | bytes 393248 | tf_op jit(solution)/shard_map/all_to_all | solution.py:259
  275.3 50.0 %gather_fusion = f32[8192]{0:T(1024)S(1)} fusion(f32[8,6144]{1,0:T(8,128)S(1)} %bitcast.262, s32[8192]{0:T(1024)S(1)} %bitcast.263), kind=kCustom, calls=%fused_computation.clone | custom fusion | bytes 131072 | tf_op jit(solution)/shard_map/jit(take_along_axis)/gather | solution.py:181
  325.5 50.0 %gather_fusion.1 = f32[8192]{0:T(1024)S(1)} fusion(f32[8,6144]{1,0:T(8,128)S(1)} %bitcast.261, s32[8192]{0:T(1024)S(1)} %bitcast.264), kind=kCustom, calls=%fused_computation.1.clone | custom fusion | bytes 131072 | tf_op jit(solution)/shard_map/jit(take_along_axis)/gather | solution.py:180
  376.3 56.7 %scatter_custom_fusion = f32[49152]{0:T(1024)S(1)} fusion(s32[8192]{0:T(1024)S(1)} %bitcast.293, f32[8192]{0:T(1024)S(1)} %bitcast.294, f32[]{:T(128)} %constant.107.clone.1), kind=kCustom, calls=%fused_computation.191 | custom fusion | flops 8192 | bytes 196612 | tf_op jit(solution)/shard_map/scatter-add | solution.py:186
  433.1 0.8 all_to_all.13
  433.9 3.5 all-to-all-start.1
  437.4 7.3 %all-to-all-done.1 = f32[4,2,6144]{2,1,0:T(2,128)S(1)} async-done(((f32[4,2,6144]{2,1,0:T(2,128)}), f32[4,2,6144]{2,1,0:T(2,128)S(1)}, u32[]{:S(2)}, u32[]{:S(2)}) %all-to-all-start.1) | async-done | bytes 196640 | tf_op jit(solution)/shard_map/all_to_all | solution.py:263
  (165 shorter events, 16.7 us)
Async XLA Ops:
  0.6 6.8 %copy-start.3 = (f32[24,16,128]{2,1,0:T(8,128)S(1)}, f32[24,16,128]{2,1,0:T(8,128)}, u32[]{:S(2)}) copy-start(f32[24,16,128]{2,1,0:T(8,128)} %param.12) | copy-start | bytes 589828
  0.6 6.8 %copy-start.2 = (f32[24,16,128]{2,1,0:T(8,128)S(1)}, f32[24,16,128]{2,1,0:T(8,128)}, u32[]{:S(2)}) copy-start(f32[24,16,128]{2,1,0:T(8,128)} %param.13) | copy-start | bytes 589828
  1.5 13.0 %collective-permute-start = (f32[2,1,16,128]{3,2,1,0:T(8,128)S(1)}, f32[2,1,16,128]{3,2,1,0:T(8,128)S(1)}, u32[]{:S(2)}, u32[]{:S(2)}) collective-permute-start(f32[2,1,16,128]{3,2,1,0:T(8,128)S(1)} %get-tuple-element.59), channel_id=1, source_target_pairs={{4,0},{8,4},{12,8},{16,12},{20,16},{24,20},{28,24},{0,28},{5,1},{9... | collective-permute-start | bytes 49160 | tf_op jit(solution)/shard_map/ppermute | solution.py:32
  7.5 7.0 %collective-permute-start.1 = (f32[2,1,16,128]{3,2,1,0:T(8,128)S(1)}, f32[2,1,16,128]{3,2,1,0:T(8,128)S(1)}, u32[]{:S(2)}, u32[]{:S(2)}) collective-permute-start(f32[2,1,16,128]{3,2,1,0:T(8,128)S(1)} %get-tuple-element.58), channel_id=1, source_target_pairs={{0,4},{4,8},{8,12},{12,16},{16,20},{20,24},{24,28},{28,0},{1,5},{5... | collective-permute-start | bytes 49160 | tf_op jit(solution)/shard_map/ppermute | solution.py:29
  7.6 5.4 %copy-start.6 = (f32[24,16,128]{2,1,0:T(8,128)S(1)}, f32[24,16,128]{2,1,0:T(8,128)}, u32[]{:S(2)}) copy-start(f32[24,16,128]{2,1,0:T(8,128)} %param.16) | copy-start | bytes 589828
  8.2 178.8 %collective-permute-start.22 = (f32[2,1,16,128]{3,1,2,0:T(1,128)}, f32[2,1,16,128]{3,1,2,0:T(1,128)S(1)}, u32[]{:S(2)}, u32[]{:S(2)}) collective-permute-start(f32[2,1,16,128]{3,1,2,0:T(1,128)} %get-tuple-element.64), channel_id=1, source_target_pairs={{0,4},{4,8},{8,12},{12,16},{16,20},{20,24},{24,28},{28,0},{1,5},{5... | collective-permute-start | bytes 49160 | tf_op jit(solution)/shard_map/ppermute | solution.py:29
  8.3 178.8 %collective-permute-start.23 = (f32[2,1,16,128]{3,1,2,0:T(1,128)}, f32[2,1,16,128]{3,1,2,0:T(1,128)}, u32[]{:S(2)}, u32[]{:S(2)}) collective-permute-start(f32[2,1,16,128]{3,1,2,0:T(1,128)} %get-tuple-element.65), channel_id=1, source_target_pairs={{4,0},{8,4},{12,8},{16,12},{20,16},{24,20},{28,24},{0,28},{5,1},{9... | collective-permute-start | bytes 49160 | tf_op jit(solution)/shard_map/ppermute | solution.py:32
  13.0 126.5 %copy-start.20 = (f32[128]{0:T(128)}, f32[128]{0:T(128)S(1)}, u32[]{:S(2)}) copy-start(f32[128]{0:T(128)S(1)} %multiply_exponential_fusion) | copy-start | bytes 1540
  14.5 1.7 collective-permute-start.2
  14.7 3.5 collective-permute-start.3
  15.1 124.4 %copy-start.23 = (f32[128]{0:T(128)}, f32[128]{0:T(128)S(1)}, u32[]{:S(2)}) copy-start(f32[128]{0:T(128)S(1)} %compare_select_fusion.4) | copy-start | bytes 1540
  18.4 3.7 collective-permute-start.4
  20.4 6.3 %collective-permute-start.5 = (f32[1,1,16,128]{3,2,1,0:T(8,128)S(1)}, f32[1,1,16,128]{3,2,1,0:T(8,128)S(1)}, u32[]{:S(2)}, u32[]{:S(2)}) collective-permute-start(f32[1,1,16,128]{3,2,1,0:T(8,128)S(1)} %get-tuple-element.94), channel_id=1, source_target_pairs={{0,4},{4,8},{8,12},{12,16},{16,20},{20,24},{24,28},{28,0},{1,5},{5... | collective-permute-start | bytes 24584 | tf_op jit(solution)/shard_map/ppermute | solution.py:29
  20.5 118.9 %copy-start.25 = (f32[128]{0:T(128)}, f32[128]{0:T(128)S(1)}, u32[]{:S(2)}) copy-start(f32[128]{0:T(128)S(1)} %pad_maximum_fusion.91) | copy-start | bytes 1540
  26.8 1.5 collective-permute-start.6
  26.9 3.2 collective-permute-start.7
  69.3 5.4 %collective-permute-start.8 = (f32[1,1,16,128]{3,2,1,0:T(8,128)S(1)}, f32[1,1,16,128]{3,2,1,0:T(8,128)S(1)}, u32[]{:S(2)}, u32[]{:S(2)}) collective-permute-start(f32[1,1,16,128]{3,2,1,0:T(8,128)S(1)} %get-tuple-element.91), channel_id=1, source_target_pairs={{4,0},{8,4},{12,8},{16,12},{20,16},{24,20},{28,24},{0,28},{5,1},{9... | collective-permute-start | bytes 24584 | tf_op jit(solution)/shard_map/ppermute | solution.py:32
  73.3 6.3 %collective-permute-start.9 = (f32[1,1,16,128]{3,2,1,0:T(8,128)S(1)}, f32[1,1,16,128]{3,2,1,0:T(8,128)S(1)}, u32[]{:S(2)}, u32[]{:S(2)}) collective-permute-start(f32[1,1,16,128]{3,2,1,0:T(8,128)S(1)} %get-tuple-element.90), channel_id=1, source_target_pairs={{0,4},{4,8},{8,12},{12,16},{16,20},{20,24},{24,28},{28,0},{1,5},{5... | collective-permute-start | bytes 24584 | tf_op jit(solution)/shard_map/ppermute | solution.py:29
  79.7 1.5 collective-permute-start.10
  79.8 3.3 collective-permute-start.11
  125.7 6.2 %collective-permute-start.12 = (f32[1,1,16,128]{3,2,1,0:T(8,128)S(1)}, f32[1,1,16,128]{3,2,1,0:T(8,128)S(1)}, u32[]{:S(2)}, u32[]{:S(2)}) collective-permute-start(f32[1,1,16,128]{3,2,1,0:T(8,128)S(1)} %get-tuple-element.87), channel_id=1, source_target_pairs={{4,0},{8,4},{12,8},{16,12},{20,16},{24,20},{28,24},{0,28},{5,1},{9... | collective-permute-start | bytes 24584 | tf_op jit(solution)/shard_map/ppermute | solution.py:32
  129.7 6.3 %collective-permute-start.13 = (f32[1,1,16,128]{3,2,1,0:T(8,128)S(1)}, f32[1,1,16,128]{3,2,1,0:T(8,128)S(1)}, u32[]{:S(2)}, u32[]{:S(2)}) collective-permute-start(f32[1,1,16,128]{3,2,1,0:T(8,128)S(1)} %get-tuple-element.86), channel_id=1, source_target_pairs={{0,4},{4,8},{8,12},{12,16},{16,20},{20,24},{24,28},{28,0},{1,5},{5... | collective-permute-start | bytes 24584 | tf_op jit(solution)/shard_map/ppermute | solution.py:29
  136.1 1.5 collective-permute-start.14
  136.2 3.3 collective-permute-start.15
  183.0 7.1 %collective-permute-start.16 = (f32[1,1,16,128]{3,2,1,0:T(8,128)S(1)}, f32[1,1,16,128]{3,2,1,0:T(8,128)S(1)}, u32[]{:S(2)}, u32[]{:S(2)}) collective-permute-start(f32[1,1,16,128]{3,2,1,0:T(8,128)S(1)} %get-tuple-element.85), channel_id=1, source_target_pairs={{4,0},{8,4},{12,8},{16,12},{20,16},{24,20},{28,24},{0,28},{5,1},{9... | collective-permute-start | bytes 24584 | tf_op jit(solution)/shard_map/ppermute | solution.py:32
  187.0 6.3 %collective-permute-start.17 = (f32[1,1,16,128]{3,2,1,0:T(8,128)S(1)}, f32[1,1,16,128]{3,2,1,0:T(8,128)S(1)}, u32[]{:S(2)}, u32[]{:S(2)}) collective-permute-start(f32[1,1,16,128]{3,2,1,0:T(8,128)S(1)} %get-tuple-element.84), channel_id=1, source_target_pairs={{0,4},{4,8},{8,12},{12,16},{16,20},{20,24},{24,28},{28,0},{1,5},{5... | collective-permute-start | bytes 24584 | tf_op jit(solution)/shard_map/ppermute | solution.py:29
  188.3 66.0 %collective-permute-start.26 = (f32[2,26,1,128]{3,1,2,0:T(8,128)}, f32[2,26,1,128]{3,1,2,0:T(8,128)}, u32[]{:S(2)}, u32[]{:S(2)}) collective-permute-start(f32[2,26,1,128]{3,1,2,0:T(8,128)} %get-tuple-element.52), channel_id=1, source_target_pairs={{0,1},{1,2},{2,3},{3,0},{4,5},{5,6},{6,7},{7,4},{8,9},{9,10},{10,1... | collective-permute-start | bytes 79880 | tf_op jit(solution)/shard_map/ppermute | solution.py:29
  188.4 66.0 %collective-permute-start.27 = (f32[2,26,1,128]{3,1,2,0:T(8,128)}, f32[2,26,1,128]{3,1,2,0:T(8,128)}, u32[]{:S(2)}, u32[]{:S(2)}) collective-permute-start(f32[2,26,1,128]{3,1,2,0:T(8,128)} %get-tuple-element.53), channel_id=1, source_target_pairs={{1,0},{2,1},{3,2},{0,3},{5,4},{6,5},{7,6},{4,7},{9,8},{10,9},{11,1... | collective-permute-start | bytes 79880 | tf_op jit(solution)/shard_map/ppermute | solution.py:32
  190.1 3.4 copy-start.16
  193.4 1.5 collective-permute-start.18
  194.0 3.1 copy-start.26
  194.0 3.1 collective-permute-start.19
  239.3 4.2 copy-start.7
  239.5 5.4 %collective-permute-start.20 = (f32[1,1,16,128]{3,2,1,0:T(8,128)S(1)}, f32[1,1,16,128]{3,2,1,0:T(8,128)S(1)}, u32[]{:S(2)}, u32[]{:S(2)}) collective-permute-start(f32[1,1,16,128]{3,2,1,0:T(8,128)S(1)} %get-tuple-element.79), channel_id=1, source_target_pairs={{4,0},{8,4},{12,8},{16,12},{20,16},{24,20},{28,24},{0,28},{5,1},{9... | collective-permute-start | bytes 24584 | tf_op jit(solution)/shard_map/ppermute | solution.py:32
  243.5 6.3 %collective-permute-start.21 = (f32[1,1,16,128]{3,2,1,0:T(8,128)S(1)}, f32[1,1,16,128]{3,2,1,0:T(8,128)S(1)}, u32[]{:S(2)}, u32[]{:S(2)}) collective-permute-start(f32[1,1,16,128]{3,2,1,0:T(8,128)S(1)} %get-tuple-element.78), channel_id=1, source_target_pairs={{0,4},{4,8},{8,12},{12,16},{16,20},{20,24},{24,28},{28,0},{1,5},{5... | collective-permute-start | bytes 24584 | tf_op jit(solution)/shard_map/ppermute | solution.py:29
  243.6 6.9 %copy-start.5 = (f32[24,16,128]{2,1,0:T(8,128)}, f32[24,16,128]{2,1,0:T(8,128)S(1)}, u32[]{:S(2)}) copy-start(f32[24,16,128]{2,1,0:T(8,128)S(1)} %get-tuple-element.42) | copy-start | bytes 589828
  249.8 1.5 collective-permute-start.24
  249.9 3.3 collective-permute-start.25
  258.6 3.8 copy-start.12
  258.6 3.8 copy-start.13
  258.6 4.1 copy-start.11
  258.6 15.8 %all-to-all-start = ((f32[4,2,12288]{2,1,0:T(2,128)}), f32[4,2,12288]{2,1,0:T(2,128)S(1)}, u32[]{:S(2)}, u32[]{:S(2)}) async-start(f32[4,2,12288]{2,1,0:T(2,128)} %fusion.110), calls=%async_computation | async-start | bytes 786432 | tf_op jit(solution)/shard_map/all_to_all | solution.py:259
  325.4 50.1 %copy-start.14 = (f32[1,1,8,1024]{3,2,1,0:T(8,128)S(1)}, f32[1,1,8,1024]{3,2,1,0:T(8,128)}, u32[]{:S(2)}) copy-start(f32[1,1,8,1024]{3,2,1,0:T(8,128)} %param.19) | copy-start | bytes 98308
  325.5 50.1 %copy-start.15 = (f32[1,1,8,1024]{3,2,1,0:T(8,128)S(1)}, f32[1,1,8,1024]{3,2,1,0:T(8,128)}, u32[]{:S(2)}) copy-start(f32[1,1,8,1024]{3,2,1,0:T(8,128)} %param.20) | copy-start | bytes 98308
  325.5 50.1 %copy-start.31 = (s32[1,1,8]{2,1,0:T(1,128)S(1)}, s32[1,1,8]{2,1,0:T(1,128)}, u32[]{:S(2)}) copy-start(s32[1,1,8]{2,1,0:T(1,128)} %param.18) | copy-start | bytes 100
  433.9 10.9 %copy-start.28 = (s32[8]{0:T(128)S(1)}, s32[8]{0:T(128)}, u32[]{:S(2)}) copy-start(s32[8]{0:T(128)} %copy-done.27) | copy-start | bytes 100
  433.9 10.9 %copy-start.30 = (s32[1,1,8]{2,1,0:T(1,128)S(1)}, s32[1,1,8]{2,1,0:T(1,128)}, u32[]{:S(2)}) copy-start(s32[1,1,8]{2,1,0:T(1,128)} %param.17) | copy-start | bytes 100
  433.9 10.8 %all-to-all-start.1 = ((f32[4,2,6144]{2,1,0:T(2,128)}), f32[4,2,6144]{2,1,0:T(2,128)S(1)}, u32[]{:S(2)}, u32[]{:S(2)}) async-start(f32[4,2,6144]{2,1,0:T(2,128)} %all_to_all.13), calls=%async_computation.1 | async-start | bytes 393216 | tf_op jit(solution)/shard_map/all_to_all | solution.py:263
  (14 other events, 21.5 us)
where the time goes:
time: 448 us; the launch traced here: 447 us
  blocking collectives  149 us (33%)
  local copies, waits for them, and re-layouts  109 us (24%)
  other arithmetic  69.3 us (15%)
  waiting for transfers between devices  61.6 us (14%)
  starting transfers between devices  40.9 us (9%)
  between operations  15.2 us (3%)
    psum x4, blocking collectives, both_sums(): lax.psum((jnp.sum(residual * residual), jnp.sum(residual * applied)), ('g...  149 us
    scatter-add x1, other arithmetic, grow_rows(): jax.ops.segment_sum(mass_change.reshape(-1), flat_cell.reshape(-1), num_s...  56.7 us
    gather x2, local copies, waits for them, and re-layouts, grow_rows(): warmth = jnp.take_along_axis(thermal_couple[:, 1], local_cell, axis=1)  50.1 us
    gather x2, local copies, waits for them, and re-layouts, grow_rows(): jnp.take_along_axis(thermal_couple[:, 0], local_cell, axis=1)  50.1 us
    ppermute x14, waiting for transfers between devices, with_halo(): lax.ppermute(lax.slice_in_dim(block, block.shape[dim] - width, None, axis...  33.7 us
    ppermute x14, starting transfers between devices, with_halo(): lax.ppermute(lax.slice_in_dim(block, 0, width, axis=dim), axis, backward)  31.1 us
    all_to_all x1, waiting for transfers between devices, on_device(): lax.all_to_all(columns, 'gx', split_axis=0, concat_axis=0, tiled=True)  11.6 us
  transfers between devices with their start and end apart: 30, of which 22 were waited for; matrix products, arithmetic and copies ran while one was open for 3% of the time, Pallas kernels for 0%

commit v1 on v0

--- a/solution.py
+++ b/solution.py
@@ -76,7 +76,7 @@
 
 def both_sums(residual, applied):
     return lax.psum(
-        (jnp.sum(residual * residual), jnp.sum(residual * applied)), ("grp", "gx", "gy")
+        lax.psum((jnp.sum(residual * residual), jnp.sum(residual * applied)), ("gx", "gy")), "grp"
     )
 
 

time: 448 us -> 423 us (0.944)
  waiting for transfers between devices: 61.6 us -> 50.8 us
  starting transfers between devices: 40.9 us -> 33 us
  blocking collectives: 149 us -> 143 us
    psum x4, blocking collectives: 149 us -> 120 us  [both_sums(): lax.psum((jnp.sum(residual * residual), jnp.sum(residual * applied)), ('g...]
    psum x0 -> x4, blocking collectives: none -> 22.2 us  [both_sums(): lax.psum(lax.psum((jnp.sum(residual * residual), jnp.sum(residual * appli...]
    ppermute x14, starting transfers between devices: 31.1 us -> 15.2 us  [with_halo(): lax.ppermute(lax.slice_in_dim(block, 0, width, axis=dim), axis, backward)]
    ppermute x14, waiting for transfers between devices: 33.7 us -> 25.1 us  [with_halo(): lax.ppermute(lax.slice_in_dim(block, block.shape[dim] - width, None, axis...]
    ppermute x14, starting transfers between devices: 2.48 us -> 10.5 us  [with_halo(): lax.ppermute(lax.slice_in_dim(block, block.shape[dim] - width, None, axis...]
where the time goes in v1:
time: 423 us; the launch traced here: 422 us
  blocking collectives  143 us (34%)
  local copies, waits for them, and re-layouts  109 us (26%)
  other arithmetic  69.3 us (16%)
  waiting for transfers between devices  50.8 us (12%)
  starting transfers between devices  33 us (8%)
  between operations  14.9 us (4%)
    psum x4, blocking collectives, both_sums(): lax.psum((jnp.sum(residual * residual), jnp.sum(residual * applied)), ('g...  120 us
    scatter-add x1, other arithmetic, grow_rows(): jax.ops.segment_sum(mass_change.reshape(-1), flat_cell.reshape(-1), num_s...  56.7 us
    gather x2, local copies, waits for them, and re-layouts, grow_rows(): warmth = jnp.take_along_axis(thermal_couple[:, 1], local_cell, axis=1)  50.1 us
    gather x2, local copies, waits for them, and re-layouts, grow_rows(): jnp.take_along_axis(thermal_couple[:, 0], local_cell, axis=1)  50.1 us
    ppermute x14, waiting for transfers between devices, with_halo(): lax.ppermute(lax.slice_in_dim(block, block.shape[dim] - width, None, axis...  25.1 us
    psum x4, blocking collectives, both_sums(): lax.psum(lax.psum((jnp.sum(residual * residual), jnp.sum(residual * appli...  22.2 us
    ppermute x14, starting transfers between devices, with_halo(): lax.ppermute(lax.slice_in_dim(block, 0, width, axis=dim), axis, backward)  15.2 us
    ppermute x14, starting transfers between devices, with_halo(): lax.ppermute(lax.slice_in_dim(block, block.shape[dim] - width, None, axis...  10.5 us
  transfers between devices with their start and end apart: 30, of which 22 were waited for; matrix products, arithmetic and copies ran while one was open for 3% of the time, Pallas kernels for 0%

profile of v1, /device:TPU:0, one launch (start us, length us, event | category | flops | bytes accessed | tf_op | source)
XLA Modules:
  0.0 421.7 jit_solution(3716670785689220768)
XLA Ops:
  0.7 0.8 pad_maximum_fusion.74
  1.5 6.0 %collective-permute-start = (f32[2,1,16,128]{3,2,1,0:T(8,128)S(1)}, f32[2,1,16,128]{3,2,1,0:T(8,128)S(1)}, u32[]{:S(2)}, u32[]{:S(2)}) collective-permute-start(f32[2,1,16,128]{3,2,1,0:T(8,128)S(1)} %get-tuple-element.67), channel_id=1, source_target_pairs={{4,0},{8,4},{12,8},{16,12},{20,16},{24,20},{28,24},{0,28},{5,1},{9... | collective-permute-start | bytes 49160 | tf_op jit(solution)/shard_map/ppermute | solution.py:32
  8.3 4.7 %collective-permute-start.23 = (f32[2,1,16,128]{3,1,2,0:T(1,128)}, f32[2,1,16,128]{3,1,2,0:T(1,128)}, u32[]{:S(2)}, u32[]{:S(2)}) collective-permute-start(f32[2,1,16,128]{3,1,2,0:T(1,128)} %get-tuple-element.73), channel_id=1, source_target_pairs={{4,0},{8,4},{12,8},{16,12},{20,16},{24,20},{28,24},{0,28},{5,1},{9... | collective-permute-start | bytes 49160 | tf_op jit(solution)/shard_map/ppermute | solution.py:32
  15.1 1.1 collective-permute-done.2
  16.2 2.0 collective-permute-done.3
  18.4 2.0 collective-permute-start.4
  20.5 1.5 collective-permute-done.4
  22.1 4.7 %collective-permute-done.5 = f32[1,1,16,128]{3,2,1,0:T(8,128)S(1)} collective-permute-done((f32[1,1,16,128]{3,2,1,0:T(8,128)S(1)}, f32[1,1,16,128]{3,2,1,0:T(8,128)S(1)}, u32[]{:S(2)}, u32[]{:S(2)}) %collective-permute-start.5) | collective-permute-done | bytes 8224 | tf_op jit(solution)/shard_map/ppermute | solution.py:29
  27.5 0.8 collective-permute-done.6
  28.3 1.8 collective-permute-done.7
  30.8 30.1 %all-reduce.15 = (f32[]{:T(128)}, f32[]{:T(128)}) all-reduce(f32[]{:T(128)} %get-tuple-element.26, f32[]{:T(128)} %get-tuple-element.25), channel_id=1, replica_groups=mesh['grp'=2,'gx'=4,'gy'=4] {'gx','gy'}, use_global_device_ids=true, to_apply=%region_1.2 | all-reduce | flops 2 | bytes 16 | tf_op jit(solution)/shard_map/psum | solution.py:79
  60.9 5.5 %all-reduce.19 = (f32[]{:T(128)}, f32[]{:T(128)}) all-reduce(f32[]{:T(128)} %get-tuple-element.33, f32[]{:T(128)} %get-tuple-element.34), channel_id=1, replica_groups=mesh['grp'=2,'gx'=4,'gy'=4] {'grp'}, use_global_device_ids=true, to_apply=%region_2.3 | all-reduce | flops 2 | bytes 16 | tf_op jit(solution)/shard_map/psum | solution.py:78
  67.9 2.0 collective-permute-start.9
  70.1 1.4 collective-permute-done.8
  71.6 2.8 collective-permute-done.9
  75.0 0.8 collective-permute-done.10
  75.8 1.8 collective-permute-done.11
  78.4 30.1 %all-reduce.14 = (f32[]{:T(128)}, f32[]{:T(128)}) all-reduce(f32[]{:T(128)} %get-tuple-element.24, f32[]{:T(128)} %get-tuple-element.23), channel_id=1, replica_groups=mesh['grp'=2,'gx'=4,'gy'=4] {'gx','gy'}, use_global_device_ids=true, to_apply=%region_7.8 | all-reduce | flops 2 | bytes 16 | tf_op jit(solution)/shard_map/psum | solution.py:79
  108.5 5.5 %all-reduce.18 = (f32[]{:T(128)}, f32[]{:T(128)}) all-reduce(f32[]{:T(128)} %get-tuple-element.31, f32[]{:T(128)} %get-tuple-element.32), channel_id=1, replica_groups=mesh['grp'=2,'gx'=4,'gy'=4] {'grp'}, use_global_device_ids=true, to_apply=%region_8.9 | all-reduce | flops 2 | bytes 16 | tf_op jit(solution)/shard_map/psum | solution.py:78
  118.8 2.0 collective-permute-start.13
  120.8 0.9 fusion.2
  123.0 2.2 collective-permute-done.13
  126.7 1.8 collective-permute-done.15
  128.5 1.5 multiply_reduce_fusion.1
  130.0 30.2 %all-reduce.13 = (f32[]{:T(128)}, f32[]{:T(128)}) all-reduce(f32[]{:T(128)} %get-tuple-element.22, f32[]{:T(128)} %get-tuple-element.21), channel_id=1, replica_groups=mesh['grp'=2,'gx'=4,'gy'=4] {'gx','gy'}, use_global_device_ids=true, to_apply=%region_13.14 | all-reduce | flops 2 | bytes 16 | tf_op jit(solution)/shard_map/psum | solution.py:79
  160.2 5.6 %all-reduce.17 = (f32[]{:T(128)}, f32[]{:T(128)}) all-reduce(f32[]{:T(128)} %get-tuple-element.29, f32[]{:T(128)} %get-tuple-element.30), channel_id=1, replica_groups=mesh['grp'=2,'gx'=4,'gy'=4] {'grp'}, use_global_device_ids=true, to_apply=%region_14.15 | all-reduce | flops 2 | bytes 16 | tf_op jit(solution)/shard_map/psum | solution.py:78
  169.4 1.0 multiply_subtract_fusion.1
  170.5 2.0 collective-permute-start.17
  172.5 1.3 pad_maximum_fusion.69
  173.8 1.7 collective-permute-start.27
  175.6 1.3 collective-permute-done.17
  178.4 2.2 collective-permute-done.19
  181.5 30.1 %all-reduce.12 = (f32[]{:T(128)}, f32[]{:T(128)}) all-reduce(f32[]{:T(128)} %get-tuple-element.20, f32[]{:T(128)} %get-tuple-element.19), channel_id=1, replica_groups=mesh['grp'=2,'gx'=4,'gy'=4] {'gx','gy'}, use_global_device_ids=true, to_apply=%region_19.20 | all-reduce | flops 2 | bytes 16 | tf_op jit(solution)/shard_map/psum | solution.py:79
  211.6 5.5 %all-reduce.16 = (f32[]{:T(128)}, f32[]{:T(128)}) all-reduce(f32[]{:T(128)} %get-tuple-element.27, f32[]{:T(128)} %get-tuple-element.28), channel_id=1, replica_groups=mesh['grp'=2,'gx'=4,'gy'=4] {'grp'}, use_global_device_ids=true, to_apply=%region_20.21 | all-reduce | flops 2 | bytes 16 | tf_op jit(solution)/shard_map/psum | solution.py:78
  221.2 2.0 collective-permute-start.21
  223.4 1.5 collective-permute-done.20
  224.8 2.8 collective-permute-done.21
  229.1 1.8 collective-permute-done.25
  232.1 0.8 copy-done.4
  232.9 1.2 fusion.10
  235.0 1.3 fusion.110
  236.3 3.8 all-to-all-start
  240.5 10.0 %all-to-all-done = f32[4,2,12288]{2,1,0:T(2,128)S(1)} async-done(((f32[4,2,12288]{2,1,0:T(2,128)}), f32[4,2,12288]{2,1,0:T(2,128)S(1)}, u32[]{:S(2)}, u32[]{:S(2)}) %all-to-all-start) | async-done | bytes 393248 | tf_op jit(solution)/shard_map/all_to_all | solution.py:259
  251.4 50.0 %gather_fusion = f32[8192]{0:T(1024)S(1)} fusion(f32[8,6144]{1,0:T(8,128)S(1)} %bitcast.262, s32[8192]{0:T(1024)S(1)} %bitcast.263), kind=kCustom, calls=%fused_computation.clone | custom fusion | bytes 131072 | tf_op jit(solution)/shard_map/jit(take_along_axis)/gather | solution.py:181
  301.6 50.0 %gather_fusion.1 = f32[8192]{0:T(1024)S(1)} fusion(f32[8,6144]{1,0:T(8,128)S(1)} %bitcast.261, s32[8192]{0:T(1024)S(1)} %bitcast.264), kind=kCustom, calls=%fused_computation.1.clone | custom fusion | bytes 131072 | tf_op jit(solution)/shard_map/jit(take_along_axis)/gather | solution.py:180
  352.4 56.7 %scatter_custom_fusion = f32[49152]{0:T(1024)S(1)} fusion(s32[8192]{0:T(1024)S(1)} %bitcast.293, f32[8192]{0:T(1024)S(1)} %bitcast.294, f32[]{:T(128)} %constant.107.clone.1), kind=kCustom, calls=%fused_computation.191 | custom fusion | flops 8192 | bytes 196612 | tf_op jit(solution)/shard_map/scatter-add | solution.py:186
  409.9 3.5 all-to-all-start.1
  413.5 6.2 %all-to-all-done.1 = f32[4,2,6144]{2,1,0:T(2,128)S(1)} async-done(((f32[4,2,6144]{2,1,0:T(2,128)}), f32[4,2,6144]{2,1,0:T(2,128)S(1)}, u32[]{:S(2)}, u32[]{:S(2)}) %all-to-all-start.1) | async-done | bytes 196640 | tf_op jit(solution)/shard_map/all_to_all | solution.py:263
  (169 shorter events, 20.1 us)
Async XLA Ops:
  0.6 6.8 %copy-start.3 = (f32[24,16,128]{2,1,0:T(8,128)S(1)}, f32[24,16,128]{2,1,0:T(8,128)}, u32[]{:S(2)}) copy-start(f32[24,16,128]{2,1,0:T(8,128)} %param.12) | copy-start | bytes 589828
  0.6 6.8 %copy-start.2 = (f32[24,16,128]{2,1,0:T(8,128)S(1)}, f32[24,16,128]{2,1,0:T(8,128)}, u32[]{:S(2)}) copy-start(f32[24,16,128]{2,1,0:T(8,128)} %param.13) | copy-start | bytes 589828
  1.5 13.0 %collective-permute-start = (f32[2,1,16,128]{3,2,1,0:T(8,128)S(1)}, f32[2,1,16,128]{3,2,1,0:T(8,128)S(1)}, u32[]{:S(2)}, u32[]{:S(2)}) collective-permute-start(f32[2,1,16,128]{3,2,1,0:T(8,128)S(1)} %get-tuple-element.67), channel_id=1, source_target_pairs={{4,0},{8,4},{12,8},{16,12},{20,16},{24,20},{28,24},{0,28},{5,1},{9... | collective-permute-start | bytes 49160 | tf_op jit(solution)/shard_map/ppermute | solution.py:32
  7.5 7.0 %collective-permute-start.1 = (f32[2,1,16,128]{3,2,1,0:T(8,128)S(1)}, f32[2,1,16,128]{3,2,1,0:T(8,128)S(1)}, u32[]{:S(2)}, u32[]{:S(2)}) collective-permute-start(f32[2,1,16,128]{3,2,1,0:T(8,128)S(1)} %get-tuple-element.66), channel_id=1, source_target_pairs={{0,4},{4,8},{8,12},{12,16},{16,20},{20,24},{24,28},{28,0},{1,5},{5... | collective-permute-start | bytes 49160 | tf_op jit(solution)/shard_map/ppermute | solution.py:29
  7.6 5.4 %copy-start.6 = (f32[24,16,128]{2,1,0:T(8,128)S(1)}, f32[24,16,128]{2,1,0:T(8,128)}, u32[]{:S(2)}) copy-start(f32[24,16,128]{2,1,0:T(8,128)} %param.16) | copy-start | bytes 589828
  8.2 164.3 %collective-permute-start.22 = (f32[2,1,16,128]{3,1,2,0:T(1,128)}, f32[2,1,16,128]{3,1,2,0:T(1,128)S(1)}, u32[]{:S(2)}, u32[]{:S(2)}) collective-permute-start(f32[2,1,16,128]{3,1,2,0:T(1,128)} %get-tuple-element.72), channel_id=1, source_target_pairs={{0,4},{4,8},{8,12},{12,16},{16,20},{20,24},{24,28},{28,0},{1,5},{5... | collective-permute-start | bytes 49160 | tf_op jit(solution)/shard_map/ppermute | solution.py:29
  8.3 164.3 %collective-permute-start.23 = (f32[2,1,16,128]{3,1,2,0:T(1,128)}, f32[2,1,16,128]{3,1,2,0:T(1,128)}, u32[]{:S(2)}, u32[]{:S(2)}) collective-permute-start(f32[2,1,16,128]{3,1,2,0:T(1,128)} %get-tuple-element.73), channel_id=1, source_target_pairs={{4,0},{8,4},{12,8},{16,12},{20,16},{24,20},{28,24},{0,28},{5,1},{9... | collective-permute-start | bytes 49160 | tf_op jit(solution)/shard_map/ppermute | solution.py:32
  13.0 115.5 %copy-start.20 = (f32[128]{0:T(128)}, f32[128]{0:T(128)S(1)}, u32[]{:S(2)}) copy-start(f32[128]{0:T(128)S(1)} %multiply_exponential_fusion) | copy-start | bytes 1540
  14.5 1.7 collective-permute-start.2
  14.7 3.5 collective-permute-start.3
  15.1 113.4 %copy-start.23 = (f32[128]{0:T(128)}, f32[128]{0:T(128)S(1)}, u32[]{:S(2)}) copy-start(f32[128]{0:T(128)S(1)} %compare_select_fusion.4) | copy-start | bytes 1540
  18.4 3.7 collective-permute-start.4
  20.4 6.3 %collective-permute-start.5 = (f32[1,1,16,128]{3,2,1,0:T(8,128)S(1)}, f32[1,1,16,128]{3,2,1,0:T(8,128)S(1)}, u32[]{:S(2)}, u32[]{:S(2)}) collective-permute-start(f32[1,1,16,128]{3,2,1,0:T(8,128)S(1)} %get-tuple-element.102), channel_id=1, source_target_pairs={{0,4},{4,8},{8,12},{12,16},{16,20},{20,24},{24,28},{28,0},{1,5},{5... | collective-permute-start | bytes 24584 | tf_op jit(solution)/shard_map/ppermute | solution.py:29
  20.5 108.0 %copy-start.25 = (f32[128]{0:T(128)}, f32[128]{0:T(128)S(1)}, u32[]{:S(2)}) copy-start(f32[128]{0:T(128)S(1)} %pad_maximum_fusion.91) | copy-start | bytes 1540
  26.8 1.5 collective-permute-start.6
  26.9 3.2 collective-permute-start.7
  67.9 3.7 collective-permute-start.8
  67.9 6.4 %collective-permute-start.9 = (f32[1,1,16,128]{3,2,1,0:T(8,128)S(1)}, f32[1,1,16,128]{3,2,1,0:T(8,128)S(1)}, u32[]{:S(2)}, u32[]{:S(2)}) collective-permute-start(f32[1,1,16,128]{3,2,1,0:T(8,128)S(1)} %get-tuple-element.98), channel_id=1, source_target_pairs={{0,4},{4,8},{8,12},{12,16},{16,20},{20,24},{24,28},{28,0},{1,5},{5... | collective-permute-start | bytes 24584 | tf_op jit(solution)/shard_map/ppermute | solution.py:29
  74.4 1.5 collective-permute-start.10
  74.4 3.2 collective-permute-start.11
  118.7 4.3 %collective-permute-start.12 = (f32[1,1,16,128]{3,2,1,0:T(8,128)S(1)}, f32[1,1,16,128]{3,2,1,0:T(8,128)S(1)}, u32[]{:S(2)}, u32[]{:S(2)}) collective-permute-start(f32[1,1,16,128]{3,2,1,0:T(8,128)S(1)} %get-tuple-element.95), channel_id=1, source_target_pairs={{4,0},{8,4},{12,8},{16,12},{20,16},{24,20},{28,24},{0,28},{5,1},{9... | collective-permute-start | bytes 24584 | tf_op jit(solution)/shard_map/ppermute | solution.py:32
  118.8 3.5 copy-start.10
  118.8 6.4 %collective-permute-start.13 = (f32[1,1,16,128]{3,2,1,0:T(8,128)S(1)}, f32[1,1,16,128]{3,2,1,0:T(8,128)S(1)}, u32[]{:S(2)}, u32[]{:S(2)}) collective-permute-start(f32[1,1,16,128]{3,2,1,0:T(8,128)S(1)} %get-tuple-element.94), channel_id=1, source_target_pairs={{0,4},{4,8},{8,12},{12,16},{16,20},{20,24},{24,28},{28,0},{1,5},{5... | collective-permute-start | bytes 24584 | tf_op jit(solution)/shard_map/ppermute | solution.py:29
  125.2 1.5 collective-permute-start.14
  125.3 3.2 collective-permute-start.15
  170.4 5.1 %collective-permute-start.16 = (f32[1,1,16,128]{3,2,1,0:T(8,128)S(1)}, f32[1,1,16,128]{3,2,1,0:T(8,128)S(1)}, u32[]{:S(2)}, u32[]{:S(2)}) collective-permute-start(f32[1,1,16,128]{3,2,1,0:T(8,128)S(1)} %get-tuple-element.93), channel_id=1, source_target_pairs={{4,0},{8,4},{12,8},{16,12},{20,16},{24,20},{28,24},{0,28},{5,1},{9... | collective-permute-start | bytes 24584 | tf_op jit(solution)/shard_map/ppermute | solution.py:32
  170.5 6.4 %collective-permute-start.17 = (f32[1,1,16,128]{3,2,1,0:T(8,128)S(1)}, f32[1,1,16,128]{3,2,1,0:T(8,128)S(1)}, u32[]{:S(2)}, u32[]{:S(2)}) collective-permute-start(f32[1,1,16,128]{3,2,1,0:T(8,128)S(1)} %get-tuple-element.92), channel_id=1, source_target_pairs={{0,4},{4,8},{8,12},{12,16},{16,20},{20,24},{24,28},{28,0},{1,5},{5... | collective-permute-start | bytes 24584 | tf_op jit(solution)/shard_map/ppermute | solution.py:29
  173.8 58.2 %collective-permute-start.26 = (f32[2,26,1,128]{3,1,2,0:T(8,128)}, f32[2,26,1,128]{3,1,2,0:T(8,128)}, u32[]{:S(2)}, u32[]{:S(2)}) collective-permute-start(f32[2,26,1,128]{3,1,2,0:T(8,128)} %get-tuple-element.60), channel_id=1, source_target_pairs={{0,1},{1,2},{2,3},{3,0},{4,5},{5,6},{6,7},{7,4},{8,9},{9,10},{10,1... | collective-permute-start | bytes 79880 | tf_op jit(solution)/shard_map/ppermute | solution.py:29
  173.8 58.2 %collective-permute-start.27 = (f32[2,26,1,128]{3,1,2,0:T(8,128)}, f32[2,26,1,128]{3,1,2,0:T(8,128)}, u32[]{:S(2)}, u32[]{:S(2)}) collective-permute-start(f32[2,26,1,128]{3,1,2,0:T(8,128)} %get-tuple-element.61), channel_id=1, source_target_pairs={{1,0},{2,1},{3,2},{0,3},{5,4},{6,5},{7,6},{4,7},{9,8},{10,9},{11,1... | collective-permute-start | bytes 79880 | tf_op jit(solution)/shard_map/ppermute | solution.py:32
  176.9 1.5 collective-permute-start.18
  177.5 3.1 copy-start.24
  177.5 3.1 copy-start.26
  177.5 3.1 collective-permute-start.19
  221.1 3.7 collective-permute-start.20
  221.2 6.4 %collective-permute-start.21 = (f32[1,1,16,128]{3,2,1,0:T(8,128)S(1)}, f32[1,1,16,128]{3,2,1,0:T(8,128)S(1)}, u32[]{:S(2)}, u32[]{:S(2)}) collective-permute-start(f32[1,1,16,128]{3,2,1,0:T(8,128)S(1)} %get-tuple-element.86), channel_id=1, source_target_pairs={{0,4},{4,8},{8,12},{12,16},{16,20},{20,24},{24,28},{28,0},{1,5},{5... | collective-permute-start | bytes 24584 | tf_op jit(solution)/shard_map/ppermute | solution.py:29
  223.4 4.9 %copy-start.5 = (f32[24,16,128]{2,1,0:T(8,128)}, f32[24,16,128]{2,1,0:T(8,128)S(1)}, u32[]{:S(2)}) copy-start(f32[24,16,128]{2,1,0:T(8,128)S(1)} %get-tuple-element.50) | copy-start | bytes 589828
  227.6 1.5 collective-permute-start.24
  227.7 3.2 collective-permute-start.25
  236.3 3.8 copy-start.12
  236.3 3.8 copy-start.13
  236.3 4.1 copy-start.11
  236.3 14.2 %all-to-all-start = ((f32[4,2,12288]{2,1,0:T(2,128)}), f32[4,2,12288]{2,1,0:T(2,128)S(1)}, u32[]{:S(2)}, u32[]{:S(2)}) async-start(f32[4,2,12288]{2,1,0:T(2,128)} %fusion.110), calls=%async_computation | async-start | bytes 786432 | tf_op jit(solution)/shard_map/all_to_all | solution.py:259
  301.5 50.1 %copy-start.14 = (f32[1,1,8,1024]{3,2,1,0:T(8,128)S(1)}, f32[1,1,8,1024]{3,2,1,0:T(8,128)}, u32[]{:S(2)}) copy-start(f32[1,1,8,1024]{3,2,1,0:T(8,128)} %param.19) | copy-start | bytes 98308
  301.5 50.1 %copy-start.15 = (f32[1,1,8,1024]{3,2,1,0:T(8,128)S(1)}, f32[1,1,8,1024]{3,2,1,0:T(8,128)}, u32[]{:S(2)}) copy-start(f32[1,1,8,1024]{3,2,1,0:T(8,128)} %param.20) | copy-start | bytes 98308
  301.5 50.1 %copy-start.31 = (s32[1,1,8]{2,1,0:T(1,128)S(1)}, s32[1,1,8]{2,1,0:T(1,128)}, u32[]{:S(2)}) copy-start(s32[1,1,8]{2,1,0:T(1,128)} %param.18) | copy-start | bytes 100
  409.9 9.9 %copy-start.28 = (s32[8]{0:T(128)S(1)}, s32[8]{0:T(128)}, u32[]{:S(2)}) copy-start(s32[8]{0:T(128)} %copy-done.27) | copy-start | bytes 100
  409.9 9.9 %copy-start.30 = (s32[1,1,8]{2,1,0:T(1,128)S(1)}, s32[1,1,8]{2,1,0:T(1,128)}, u32[]{:S(2)}) copy-start(s32[1,1,8]{2,1,0:T(1,128)} %param.17) | copy-start | bytes 100
  409.9 9.7 %all-to-all-start.1 = ((f32[4,2,6144]{2,1,0:T(2,128)}), f32[4,2,6144]{2,1,0:T(2,128)S(1)}, u32[]{:S(2)}, u32[]{:S(2)}) async-start(f32[4,2,6144]{2,1,0:T(2,128)} %all_to_all.13), calls=%async_computation.1 | async-start | bytes 393216 | tf_op jit(solution)/shard_map/all_to_all | solution.py:263
  (14 other events, 20.5 us)
